TPU v7x, 256 devices: a whole 4x4x8 slice. The times are simulated.
256 devices in a mesh: row: 16 (over y, x), col: 16 (over z, core).
Axes of the slice: x: 4, y: 4, z: 8, core: 2. Of those that a mesh axis runs over, the one named last changes fastest.
Arguments:
- diag_inv: float32 [2, 2048, 2048], P(None, 'col', 'row'), may hold values from -0.125 to 0.125
- cross_block: float32 [2048, 2048], P('row', 'col'), may hold values from -0.125 to 0.125
- coupling: float32 [2, 2048, 65536], P(None, 'row', 'col'), may hold values from -0.125 to 0.125
- panel_loads: float32 [2, 1024, 2048], P(None, 'row', 'col'), may hold values from -6 to 6
- rest_loads: float32 [1024, 65536], P('row', 'col'), may hold values from -6 to 6
Outputs:
- solved: float32 [2, 1024, 2048], P(None, None, 'row')
- rest_updated: float32 [1024, 65536], P('row', 'col')
All inputs are finite; a program needn't handle non-finite values.
Results may differ from a plain program's by a relative error of at most 0.00008.
Values sent between devices are 32-bit elements; how exact they have to be, the bound alone decides.
A program may use at most 128 MiB of HBM per device.

v0:
```python
import jax
import jax.numpy as jnp
from jax import lax
from jax.sharding import PartitionSpec as P


def product(left, right):
    return jnp.dot(left, right, precision=lax.Precision.HIGHEST, preferred_element_type=jnp.float32)


def local(diag_inv, cross_block, coupling, panel_loads, rest_loads):
    both_full = lax.all_gather(panel_loads, "row", axis=1, tiled=True)

    def solve_panel(loads_full, panel_index):
        partial_value = product(loads_full, diag_inv[panel_index])
        return lax.psum(partial_value, "col")

    upper_solved = solve_panel(both_full[1], 1)
    lower_local = panel_loads[0] - lax.psum_scatter(
        product(upper_solved, cross_block), "row", scatter_dimension=0, tiled=True
    )
    lower_full = lax.all_gather(lower_local, "row", axis=0, tiled=True)
    lower_solved = solve_panel(lower_full, 0)

    def apply_panel(current, solved_part, panel_index):
        return current - lax.psum_scatter(
            product(solved_part, coupling[panel_index]), "row", scatter_dimension=0, tiled=True
        )

    rest_updated = apply_panel(rest_loads, upper_solved, 1)
    rest_updated = apply_panel(rest_updated, lower_solved, 0)
    return (jnp.stack([lower_solved, upper_solved]), rest_updated)


def solution(mesh):
    in_specs = (
        P(None, "col", "row"),
        P("row", "col"),
        P(None, "row", "col"),
        P(None, "row", "col"),
        P("row", "col"),
    )
    out_specs = (P(None, None, "row"), P("row", "col"))
    return jax.shard_map(local, mesh=mesh, in_specs=in_specs, out_specs=out_specs, check_vma=False)
```

profile of v0, /device:TPU:1, one launch (start us, length us, event | category | flops | bytes accessed | tf_op | source)
XLA Modules:
  0.0 639.2 jit_solution(14545961122653395243)
XLA Ops:
  7.2 0.0 copy-start
  7.2 0.0 all-gather.2.cloned.1.call-start
  7.2 0.7 all-gather.2.cloned.1.call-update
  7.9 0.0 all-reduce.3.cloned.1.call-start
  8.0 52.6 %all-gather.2.cloned.1.call-done = f32[2,1024,128]{2,1,0:T(8,128)} async-done(((f32[2,64,128]{2,1,0:T(8,128)}), f32[2,1024,128]{2,1,0:T(8,128)}) %all-gather.2.cloned.1.call-update) | async-done | bytes 1048592 | tf_op jit(solution)/shard_map/all_gather | solution.py:12
  60.6 2.4 fusion.6
  63.0 0.0 all-reduce.3.cloned.1.call-update
  63.0 0.0 reduce-scatter.4.cloned.1.call-start
  63.0 110.8 %all-reduce.3.cloned.1.call-done = f32[1024,128]{1,0:T(8,128)} async-done(((f32[1024,128]{1,0:T(8,128)}), f32[1024,128]{1,0:T(8,128)}) %all-reduce.3.cloned.1.call-update) | async-done | bytes 524304 | tf_op jit(solution)/shard_map/psum | solution.py:16
  173.8 0.0 copy-done
  173.8 2.5 fusion.12
  176.3 0.0 reduce-scatter.4.cloned.1.call-update
  176.3 0.0 all-reduce.5.cloned.1.call-start
  176.4 78.0 %reduce-scatter.4.cloned.1.call-done = f32[64,128]{1,0:T(8,128)} async-done(((f32[1024,128]{1,0:T(8,128)}), f32[64,128]{1,0:T(8,128)}) %reduce-scatter.4.cloned.1.call-update) | async-done | bytes 32784 | tf_op jit(solution)/shard_map/reduce_scatter | solution.py:19
  254.3 0.8 bitcast_subtract_fusion
  255.1 17.5 %all_gather.7 = f32[1024,128]{1,0:T(8,128)S(1)} all-gather(f32[64,128]{1,0:T(8,128)S(1)} %bitcast_subtract_fusion), channel_id=1, replica_groups=mesh['row'=16,'col'=16] {'row'}, dimensions={0}, use_global_device_ids=true | all-gather | bytes 557056 | tf_op jit(solution)/shard_map/all_gather | solution.py:22
  272.6 2.2 fusion.7
  274.8 0.0 all-reduce.5.cloned.1.call-update
  274.8 0.0 reduce-scatter.6.cloned.1.call-start
  274.9 0.0 copy-done.1
  274.9 16.7 %fusion.2 = f32[1024,4096]{1,0:T(8,128)} fusion(f32[1024,128]{1,0:T(8,128)S(1)} %copy-done.1, f32[2,128,4096]{2,1,0:T(8,128)} %param.7), kind=kOutput, calls=%fused_computation.2 | convolution fusion | flops 6442450944 | bytes 19398656 | tf_op jit(solution)/shard_map/dot_general | solution.py:8
  291.6 0.0 reduce-scatter.6.cloned.1.call-update
  291.6 0.0 reduce-scatter.8.cloned.1.call-start
  291.7 99.1 %all-reduce.5.cloned.1.call-done = f32[1024,128]{1,0:T(8,128)} async-done(((f32[1024,128]{1,0:T(8,128)}), f32[1024,128]{1,0:T(8,128)}) %all-reduce.5.cloned.1.call-update) | async-done | bytes 524304 | tf_op jit(solution)/shard_map/psum | solution.py:16
  390.8 17.1 %fusion = f32[1024,4096]{1,0:T(8,128)} fusion(f32[1024,128]{1,0:T(8,128)} %all-reduce.5.cloned.1.call-done, f32[2,128,4096]{2,1,0:T(8,128)} %param.7), kind=kOutput, calls=%fused_computation | convolution fusion | flops 6442450944 | bytes 19398656 | tf_op jit(solution)/shard_map/dot_general | solution.py:8
  407.9 0.0 reduce-scatter.8.cloned.1.call-update
  407.9 1.0 copy-done.2
  408.9 1.0 pad_maximum_fusion
  410.0 100.4 %reduce-scatter.6.cloned.1.call-done = f32[64,4096]{1,0:T(8,128)} async-done(((f32[1024,4096]{1,0:T(8,128)}), f32[64,4096]{1,0:T(8,128)}) %reduce-scatter.6.cloned.1.call-update) | async-done | bytes 1048592 | tf_op jit(solution)/shard_map/reduce_scatter | solution.py:26
  510.4 119.3 %reduce-scatter.8.cloned.1.call-done = f32[64,4096]{1,0:T(8,128)} async-done(((f32[1024,4096]{1,0:T(8,128)}), f32[64,4096]{1,0:T(8,128)}) %reduce-scatter.8.cloned.1.call-update) | async-done | bytes 1048592 | tf_op jit(solution)/shard_map/reduce_scatter | solution.py:26
  629.7 0.0 copy-done.3
  629.7 2.7 subtract_subtract_fusion
  (3 shorter events, 0.0 us)
Async XLA Ops:
  7.2 166.6 %copy-start = (f32[128,128]{1,0:T(8,128)S(1)}, f32[128,128]{1,0:T(8,128)}, u32[]{:S(2)}) copy-start(f32[128,128]{1,0:T(8,128)} %param.6) | copy-start | bytes 196612
  7.2 53.4 %all-gather.2.cloned.1.call-start = ((), (), s32[]{:S(2)}) async-start(), calls=%async_computation.3 | async-start | bytes 1114112 | tf_op jit(solution)/shard_map/all_gather | solution.py:12
  7.9 165.9 %all-reduce.3.cloned.1.call-start = ((), (), s32[]{:S(2)}) async-start(), calls=%async_computation.4 | async-start | bytes 1048576 | tf_op jit(solution)/shard_map/psum | solution.py:16
  63.0 191.3 %reduce-scatter.4.cloned.1.call-start = ((), (), s32[]{:S(2)}) async-start(), calls=%async_computation.5 | async-start | bytes 557056 | tf_op jit(solution)/shard_map/reduce_scatter | solution.py:19
  173.8 101.1 %copy-start.1 = (f32[1024,128]{1,0:T(8,128)S(1)}, f32[1024,128]{1,0:T(8,128)}, u32[]{:S(2)}) copy-start(f32[1024,128]{1,0:T(8,128)} %all-reduce.3.cloned.1.call-done) | copy-start | bytes 1572868
  176.3 214.5 %all-reduce.5.cloned.1.call-start = ((), (), s32[]{:S(2)}) async-start(), calls=%async_computation.6 | async-start | bytes 1048576 | tf_op jit(solution)/shard_map/psum | solution.py:16
  274.8 235.6 %reduce-scatter.6.cloned.1.call-start = ((), (), s32[]{:S(2)}) async-start(), calls=%async_computation.7 | async-start | bytes 17825792 | tf_op jit(solution)/shard_map/reduce_scatter | solution.py:26
  291.6 338.1 %reduce-scatter.8.cloned.1.call-start = ((), (), s32[]{:S(2)}) async-start(), calls=%async_computation.8 | async-start | bytes 17825792 | tf_op jit(solution)/shard_map/reduce_scatter | solution.py:26
  407.9 1.1 copy-start.2
  407.9 221.9 %copy-start.3 = (f32[64,4096]{1,0:T(8,128)S(1)}, f32[64,4096]{1,0:T(8,128)}, u32[]{:S(2)}) copy-start(f32[64,4096]{1,0:T(8,128)} %param.9) | copy-start | bytes 3145732
Sparse Core Ops, SparseCore 0:
  10.5 50.0 all-gather.1
  63.5 110.3 all-reduce.2
  178.3 76.0 reduce-scatter.3
  274.9 115.7 all-reduce.4
  394.8 115.5 reduce-scatter.5
  514.4 115.2 reduce-scatter.7
where the time goes:
time: 640 us; the launch traced here: 639 us
  waiting for transfers between devices  561 us (88%)
  matrix products  40.9 us (6%)
  blocking collectives  17.5 us (3%)
  between operations  14.1 us (2%)
    reduce_scatter x2, waiting for transfers between devices, apply_panel(): lax.psum_scatter(product(solved_part, coupling[panel_index]), 'row', scat...  220 us
    psum x2, waiting for transfers between devices, solve_panel(): return lax.psum(partial_value, 'col')  210 us
    reduce_scatter x1, waiting for transfers between devices, local(): lax.psum_scatter(product(upper_solved, cross_block), 'row', scatter_dimen...  78 us
    all_gather x1, waiting for transfers between devices, local(): both_full = lax.all_gather(panel_loads, 'row', axis=1, tiled=True)  52.6 us
    dot_general x5, matrix products, product(): jnp.dot(left, right, precision=lax.Precision.HIGHEST, preferred_element_t...  40.9 us
    all_gather x1, blocking collectives, local(): lower_full = lax.all_gather(lower_local, 'row', axis=0, tiled=True)  17.5 us
  transfers between devices with their start and end apart: 6, of which 6 were waited for; matrix products, arithmetic and copies ran while one was open for 5% of the time, Pallas kernels for 0%

commit v1 on v0

--- a/solution.py
+++ b/solution.py
@@ -1,7 +1,15 @@
+import functools
 import jax
 import jax.numpy as jnp
 from jax import lax
 from jax.sharding import PartitionSpec as P
+
+
+def choose_clusters(xin, row_axis):
+    return lax.all_gather(xin, axis_name=row_axis).sum(axis=0)
+
+
+works_save = functools.partial(choose_clusters, row_axis="col")
 
 
 def product(left, right):
@@ -13,7 +21,7 @@
 
     def solve_panel(loads_full, panel_index):
         partial_value = product(loads_full, diag_inv[panel_index])
-        return lax.psum(partial_value, "col")
+        return works_save(partial_value)
 
     upper_solved = solve_panel(both_full[1], 1)
     lower_local = panel_loads[0] - lax.psum_scatter(

time: 640 us -> 528 us (0.82)
  waiting for transfers between devices: 561 us -> 445 us
  other arithmetic: 4.48 us -> 12.2 us
    psum x2 -> x0, waiting for transfers between devices: 210 us -> none  [solve_panel(): return lax.psum(partial_value, 'col')]
    all_gather x0 -> x2, waiting for transfers between devices: none -> 103 us  [choose_clusters(): return lax.all_gather(xin, axis_name=row_axis).sum(axis=0)]
    reduce_sum x0 -> x2, other arithmetic: none -> 7.69 us  [choose_clusters(): return lax.all_gather(xin, axis_name=row_axis).sum(axis=0)]
  transfers between devices with their start and end apart: 6 -> 6, of which waited for: 6 -> 6; matrix products, arithmetic and copies ran while one was open for 5% -> 7% of each run, Pallas kernels for 0% -> 0%
where the time goes in v1:
time: 528 us
  waiting for transfers between devices  445 us (84%)
  matrix products  38.6 us (7%)
  blocking collectives  17.5 us (3%)
  between operations  14.1 us (3%)
  other arithmetic  12.2 us (2%)
    reduce_scatter x2, waiting for transfers between devices, apply_panel(): lax.psum_scatter(product(solved_part, coupling[panel_index]), 'row', scat...  215 us
    all_gather x2, waiting for transfers between devices, choose_clusters(): return lax.all_gather(xin, axis_name=row_axis).sum(axis=0)  103 us
    reduce_scatter x1, waiting for transfers between devices, local(): lax.psum_scatter(product(upper_solved, cross_block), 'row', scatter_dimen...  73.9 us
    all_gather x1, waiting for transfers between devices, local(): both_full = lax.all_gather(panel_loads, 'row', axis=1, tiled=True)  52.6 us
    dot_general x5, matrix products, product(): jnp.dot(left, right, precision=lax.Precision.HIGHEST, preferred_element_t...  38.6 us
    all_gather x1, blocking collectives, local(): lower_full = lax.all_gather(lower_local, 'row', axis=0, tiled=True)  17.5 us
  transfers between devices with their start and end apart: 6, of which 6 were waited for; matrix products, arithmetic and copies ran while one was open for 7% of the time, Pallas kernels for 0%

profile of v1, /device:TPU:1, one launch (start us, length us, event | category | flops | bytes accessed | tf_op | source)
XLA Modules:
  0.0 528.0 jit_solution(8853954667262091860)
XLA Ops:
  7.2 0.0 copy-start
  7.2 0.0 all-gather.6.cloned.1.call-start
  7.2 0.7 all-gather.6.cloned.1.call-update
  7.9 0.0 all-gather.8.cloned.1.call-start
  8.0 52.6 %all-gather.6.cloned.1.call-done = f32[2,1024,128]{2,1,0:T(8,128)} async-done(((f32[2,64,128]{2,1,0:T(8,128)}), f32[2,1024,128]{2,1,0:T(8,128)}) %all-gather.6.cloned.1.call-update) | async-done | bytes 1048592 | tf_op jit(solution)/shard_map/all_gather | solution.py:20
  60.6 2.4 fusion.6
  63.0 0.0 all-gather.8.cloned.1.call-update
  63.0 0.0 reduce-scatter.4.cloned.1.call-start
  63.0 57.2 %all-gather.8.cloned.1.call-done = f32[16384,128]{1,0:T(8,128)} async-done(((f32[1024,128]{1,0:T(8,128)}), f32[16384,128]{1,0:T(8,128)}) %all-gather.8.cloned.1.call-update) | async-done | bytes 8388624 | tf_op jit(solution)/shard_map/all_gather | solution.py:9
  120.2 3.9 reduce_sum.18
  124.1 1.4 fusion.12
  125.5 0.0 reduce-scatter.4.cloned.1.call-update
  125.5 0.0 all-gather.10.cloned.1.call-start
  125.5 73.9 %reduce-scatter.4.cloned.1.call-done = f32[64,128]{1,0:T(8,128)} async-done(((f32[1024,128]{1,0:T(8,128)}), f32[64,128]{1,0:T(8,128)}) %reduce-scatter.4.cloned.1.call-update) | async-done | bytes 32784 | tf_op jit(solution)/shard_map/reduce_scatter | solution.py:27
  199.4 0.8 bitcast_subtract_fusion
  200.2 17.5 %all_gather.21 = f32[1024,128]{1,0:T(8,128)S(1)} all-gather(f32[64,128]{1,0:T(8,128)S(1)} %bitcast_subtract_fusion), channel_id=1, replica_groups=mesh['row'=16,'col'=16] {'row'}, dimensions={0}, use_global_device_ids=true | all-gather | bytes 557056 | tf_op jit(solution)/shard_map/all_gather | solution.py:30
  217.7 0.0 copy-done.3
  217.7 1.4 fusion.7
  219.0 0.0 all-gather.10.cloned.1.call-update
  219.1 0.0 reduce-scatter.6.cloned.1.call-start
  219.1 16.7 %fusion.2 = f32[1024,4096]{1,0:T(8,128)} fusion(f32[1024,128]{1,0:T(8,128)S(1)} %reduce_sum.18, f32[2,128,4096]{2,1,0:T(8,128)} %param.7), kind=kOutput, calls=%fused_computation.2 | convolution fusion | flops 6442450944 | bytes 19398656 | tf_op jit(solution)/shard_map/dot_general | solution.py:16
  235.9 0.0 reduce-scatter.6.cloned.1.call-update
  235.9 0.0 reduce-scatter.8.cloned.1.call-start
  235.9 45.8 %all-gather.10.cloned.1.call-done = f32[16384,128]{1,0:T(8,128)} async-done(((f32[1024,128]{1,0:T(8,128)}), f32[16384,128]{1,0:T(8,128)}) %all-gather.10.cloned.1.call-update) | async-done | bytes 8388624 | tf_op jit(solution)/shard_map/all_gather | solution.py:9
  281.8 3.8 reduce_sum.19
  285.6 16.7 %fusion = f32[1024,4096]{1,0:T(8,128)} fusion(f32[1024,128]{1,0:T(8,128)S(1)} %reduce_sum.19, f32[2,128,4096]{2,1,0:T(8,128)} %param.7), kind=kOutput, calls=%fused_computation | convolution fusion | flops 6442450944 | bytes 19398656 | tf_op jit(solution)/shard_map/dot_general | solution.py:16
  302.3 0.0 reduce-scatter.8.cloned.1.call-update
  302.3 1.0 pad_maximum_fusion
  303.4 95.8 %reduce-scatter.6.cloned.1.call-done = f32[64,4096]{1,0:T(8,128)} async-done(((f32[1024,4096]{1,0:T(8,128)}), f32[64,4096]{1,0:T(8,128)}) %reduce-scatter.6.cloned.1.call-update) | async-done | bytes 1048592 | tf_op jit(solution)/shard_map/reduce_scatter | solution.py:34
  399.2 119.4 %reduce-scatter.8.cloned.1.call-done = f32[64,4096]{1,0:T(8,128)} async-done(((f32[1024,4096]{1,0:T(8,128)}), f32[64,4096]{1,0:T(8,128)}) %reduce-scatter.8.cloned.1.call-update) | async-done | bytes 1048592 | tf_op jit(solution)/shard_map/reduce_scatter | solution.py:34
  518.5 0.0 copy-done.1
  518.5 2.7 subtract_subtract_fusion
  (5 shorter events, 0.0 us)
Async XLA Ops:
  7.2 116.9 %copy-start = (f32[128,128]{1,0:T(8,128)S(1)}, f32[128,128]{1,0:T(8,128)}, u32[]{:S(2)}) copy-start(f32[128,128]{1,0:T(8,128)} %param.6) | copy-start | bytes 196612
  7.2 53.4 %all-gather.6.cloned.1.call-start = ((), (), s32[]{:S(2)}) async-start(), calls=%async_computation.3 | async-start | bytes 1114112 | tf_op jit(solution)/shard_map/all_gather | solution.py:20
  7.9 112.3 %all-gather.8.cloned.1.call-start = ((), (), s32[]{:S(2)}) async-start(), calls=%async_computation.7 | async-start | bytes 8912896 | tf_op jit(solution)/shard_map/all_gather | solution.py:9
  63.0 136.4 %reduce-scatter.4.cloned.1.call-start = ((), (), s32[]{:S(2)}) async-start(), calls=%async_computation.4 | async-start | bytes 557056 | tf_op jit(solution)/shard_map/reduce_scatter | solution.py:27
  120.2 79.2 %copy-start.2 = (f32[2,64,128]{2,1,0:T(8,128)S(1)}, f32[2,64,128]{2,1,0:T(8,128)}, u32[]{:S(2)}) copy-start(f32[2,64,128]{2,1,0:T(8,128)} %param.8) | copy-start | bytes 196612
  120.2 97.5 %copy-start.3 = (f32[2,128,128]{2,1,0:T(8,128)S(1)}, f32[2,128,128]{2,1,0:T(8,128)}, u32[]{:S(2)}) copy-start(f32[2,128,128]{2,1,0:T(8,128)} %param.5) | copy-start | bytes 393220
  125.5 156.3 %all-gather.10.cloned.1.call-start = ((), (), s32[]{:S(2)}) async-start(), calls=%async_computation.8 | async-start | bytes 8912896 | tf_op jit(solution)/shard_map/all_gather | solution.py:9
  219.1 180.1 %reduce-scatter.6.cloned.1.call-start = ((), (), s32[]{:S(2)}) async-start(), calls=%async_computation.5 | async-start | bytes 17825792 | tf_op jit(solution)/shard_map/reduce_scatter | solution.py:34
  235.9 282.6 %reduce-scatter.8.cloned.1.call-start = ((), (), s32[]{:S(2)}) async-start(), calls=%async_computation.6 | async-start | bytes 17825792 | tf_op jit(solution)/shard_map/reduce_scatter | solution.py:34
  302.3 216.2 %copy-start.1 = (f32[64,4096]{1,0:T(8,128)S(1)}, f32[64,4096]{1,0:T(8,128)}, u32[]{:S(2)}) copy-start(f32[64,4096]{1,0:T(8,128)} %param.9) | copy-start | bytes 3145732
Sparse Core Ops, SparseCore 0:
  10.5 50.0 all-gather.5
  63.1 57.0 all-gather.7
  125.6 73.7 reduce-scatter.3
  219.2 62.5 all-gather.9
  285.7 113.3 reduce-scatter.5
  403.2 115.3 reduce-scatter.7
